TPU v7x, 256 devices: a whole 4x4x8 slice. The times are simulated.
256 devices in a mesh: section: 64 (over y, z, core), dp: 4 (over x).
Axes of the slice: x: 4, y: 4, z: 8, core: 2. Of those that a mesh axis runs over, the one named last changes fastest.
Arguments:
- tokens: bfloat16 [1024, 8192], P(('section', 'dp')), may hold values from -6 to 6
- norm_gain: float32 [8192], replicated, may hold values from 0.1 to 1.9
- gate_weight: bfloat16 [8192, 28672], P('dp', 'section'), may hold values from -0.0625 to 0.0625
- up_weight: bfloat16 [8192, 28672], P('dp', 'section'), may hold values from -0.0625 to 0.0625
- down_weight: bfloat16 [28672, 8192], P('section', 'dp'), may hold values from -0.03125 to 0.03125
Outputs:
- mixed: bfloat16 [1024, 8192], P(('section', 'dp'))
All inputs are finite; a program needn't handle non-finite values.
Results may differ from a plain program's by a relative error of at most 0.0046.
Values may be sent and summed in bfloat16 or wider, within the bound.
No kernel may reach another device: no remote copies, remote signals or barrier semaphores. Data moves between devices by JAX's collectives and lax.ppermute only.
A program may use at most 128 MiB of HBM per device.

v0:
```python
import jax
import jax.numpy as jnp
from jax import lax
from jax.sharding import PartitionSpec as P


def local(tokens, norm_gain, gate_weight, up_weight, down_weight):
    widened = tokens.astype(jnp.float32)
    mean_square = jnp.mean(widened * widened, axis=1, keepdims=True)
    normed_own = (widened * lax.rsqrt(mean_square + 1e-05) * norm_gain[None, :]).astype(
        jnp.bfloat16
    )
    normed = lax.all_gather(normed_own, "section", axis=0, tiled=True)
    full_gate, full_up, full_down = (
        lax.all_gather(gate_weight, "dp", axis=0, tiled=True),
        lax.all_gather(up_weight, "dp", axis=0, tiled=True),
        lax.all_gather(down_weight, "dp", axis=1, tiled=True),
    )
    gate_part = jnp.dot(normed, full_gate, preferred_element_type=jnp.float32)
    up_part = jnp.dot(normed, full_up, preferred_element_type=jnp.float32)
    hidden = (jax.nn.silu(gate_part) * up_part).astype(jnp.bfloat16)
    summed = lax.psum_scatter(
        jnp.dot(hidden, full_down, preferred_element_type=jnp.float32),
        "section",
        scatter_dimension=0,
        tiled=True,
    )
    return (widened + summed).astype(jnp.bfloat16)


def solution(mesh):
    return jax.shard_map(
        local,
        mesh=mesh,
        in_specs=(
            P(("section", "dp"), None),
            P(),
            P("dp", "section"),
            P("dp", "section"),
            P("section", "dp"),
        ),
        out_specs=P(("section", "dp"), None),
        check_vma=False,
    )
```

profile of v0, /device:TPU:2, one launch (start us, length us, event | category | flops | bytes accessed | tf_op | source)
XLA Modules:
  0.0 550.5 jit_solution(717318222495191974)
XLA Ops:
  6.5 1.0 fusion.1
  7.6 1.6 fusion.5
  9.1 0.0 all-gather.12.cloned.1.call-update
  9.2 0.0 all-gather.6.cloned.1.call-start
  9.2 0.7 all-gather.6.cloned.1.call-update
  9.9 0.0 all-gather.8.cloned.1.call-start
  10.0 0.7 all-gather.8.cloned.1.call-update
  10.7 0.0 all-gather.10.cloned.1.call-start
  10.7 0.5 all-gather.10.cloned.1.call-update
  11.2 0.0 all-reduce.3.cloned.1.call-start
  11.3 80.9 %all-gather.12.cloned.1.call-done = bf16[64,4,8192]{2,1,0:T(4,128)(2,1)} async-done(((bf16[1,4,8192]{2,1,0:T(4,128)(2,1)}), bf16[64,4,8192]{2,1,0:T(4,128)(2,1)}) %all-gather.12.cloned.1.call-update) | async-done | bytes 4194320 | tf_op jit(solution)/shard_map/all_gather | solution.py:13
  92.2 6.9 %reshape.10 = bf16[256,8192]{1,0:T(8,128)(2,1)} reshape(bf16[64,4,8192]{2,1,0:T(4,128)(2,1)} %all-gather.12.cloned.1.call-done) | data formatting | bytes 8388608
  99.1 69.0 %all-gather.6.cloned.1.call-done = bf16[8192,448]{0,1:T(8,128)(2,1)} async-done(((bf16[2048,448]{0,1:T(8,128)(2,1)}), bf16[8192,448]{0,1:T(8,128)(2,1)}) %all-gather.6.cloned.1.call-update) | async-done | bytes 7340048 | tf_op jit(solution)/shard_map/all_gather | solution.py:15
  168.1 6.4 %fusion.6 = f32[256,448]{0,1:T(8,128)S(1)} fusion(bf16[256,8192]{1,0:T(8,128)(2,1)} %reshape.10, bf16[8192,448]{0,1:T(8,128)(2,1)} %all-gather.6.cloned.1.call-done), kind=kOutput, calls=%fused_computation.11 | convolution fusion | flops 1879048192 | bytes 11993088 | tf_op jit(solution)/shard_map/dot_general | solution.py:19
  174.5 73.2 %all-gather.8.cloned.1.call-done = bf16[8192,448]{0,1:T(8,128)(2,1)} async-done(((bf16[2048,448]{0,1:T(8,128)(2,1)}), bf16[8192,448]{0,1:T(8,128)(2,1)}) %all-gather.8.cloned.1.call-update) | async-done | bytes 7340048 | tf_op jit(solution)/shard_map/all_gather | solution.py:16
  247.7 6.5 %fusion = bf16[256,448]{0,1:T(8,128)(2,1)S(1)} fusion(bf16[256,8192]{1,0:T(8,128)(2,1)} %reshape.10, bf16[8192,448]{0,1:T(8,128)(2,1)} %all-gather.8.cloned.1.call-done, f32[256,448]{0,1:T(8,128)S(1)} %fusion.6), kind=kOutput, calls=%fused_computation.1 | convolution fusion | flops 1879736320 | bytes 12222464 | tf_op jit(solution)/shard_map/dot_general | solution.py:20
  254.2 73.0 %all-gather.10.cloned.1.call-done = bf16[448,8192]{1,0:T(8,128)(2,1)} async-done(((bf16[448,2048]{1,0:T(8,128)(2,1)}), bf16[448,8192]{1,0:T(8,128)(2,1)}) %all-gather.10.cloned.1.call-update) | async-done | bytes 7340048 | tf_op jit(solution)/shard_map/all_gather | solution.py:17
  327.2 8.8 %fusion.7 = f32[256,8192]{1,0:T(8,128)} fusion(bf16[256,448]{0,1:T(8,128)(2,1)S(1)} %fusion, bf16[448,8192]{1,0:T(8,128)(2,1)} %all-gather.10.cloned.1.call-done), kind=kOutput, calls=%fused_computation.12 | convolution fusion | flops 1879048192 | bytes 15958016 | tf_op jit(solution)/shard_map/dot_general | solution.py:23
  336.0 0.0 all-reduce.3.cloned.1.call-update
  336.0 0.6 copy-done.1
  336.6 0.6 dynamic-slice
  337.9 204.5 %all-reduce.3.cloned.1.call-done = f32[256,8192]{1,0:T(8,128)} async-done(((f32[256,8192]{1,0:T(8,128)}), f32[256,8192]{1,0:T(8,128)}) %all-reduce.3.cloned.1.call-update) | async-done | bytes 8388624
  542.4 0.0 copy-done
  542.4 1.6 fusion.4
  (4 shorter events, 0.0 us)
Async XLA Ops:
  6.5 85.6 %all-gather.12.cloned.1.call-start = ((), (), s32[]{:S(2)}) async-start(), calls=%async_computation.3 | async-start | bytes 4259840 | tf_op jit(solution)/shard_map/all_gather | solution.py:13
  9.2 158.9 %all-gather.6.cloned.1.call-start = ((), (), s32[]{:S(2)}) async-start(), calls=%async_computation | async-start | bytes 9175040 | tf_op jit(solution)/shard_map/all_gather | solution.py:15
  9.9 237.8 %all-gather.8.cloned.1.call-start = ((), (), s32[]{:S(2)}) async-start(), calls=%async_computation.1 | async-start | bytes 9175040 | tf_op jit(solution)/shard_map/all_gather | solution.py:16
  10.7 316.5 %all-gather.10.cloned.1.call-start = ((), (), s32[]{:S(2)}) async-start(), calls=%async_computation.2 | async-start | bytes 9175040 | tf_op jit(solution)/shard_map/all_gather | solution.py:17
  11.2 531.1 %all-reduce.3.cloned.1.call-start = ((), (), s32[]{:S(2)}) async-start(), calls=%async_computation.4 | async-start | bytes 16777216
  336.0 0.7 copy-start.1
  336.0 206.4 %copy-start = (bf16[4,8192]{1,0:T(4,128)(2,1)S(1)}, bf16[4,8192]{1,0:T(4,128)(2,1)}, u32[]{:S(2)}) copy-start(bf16[4,8192]{1,0:T(4,128)(2,1)} %param.5) | copy-start | bytes 196612
Sparse Core Ops, SparseCore 0:
  10.1 81.9 all-gather.11
  94.0 74.0 all-gather.5
  169.9 77.7 all-gather.7
  249.4 77.7 all-gather.9
  336.1 206.2 all-reduce.2
where the time goes:
time: 551 us
  waiting for transfers between devices  503 us (91%)
  matrix products  21.7 us (4%)
  between operations  13.8 us (3%)
  local copies, waits for them, and re-layouts  8.13 us (1%)
    unnamed x6, waiting for transfers between devices  206 us
    all_gather x1, waiting for transfers between devices, local(): normed = lax.all_gather(normed_own, 'section', axis=0, tiled=True)  80.9 us
    all_gather x1, waiting for transfers between devices, local(): lax.all_gather(up_weight, 'dp', axis=0, tiled=True)  73.2 us
    all_gather x1, waiting for transfers between devices, local(): lax.all_gather(down_weight, 'dp', axis=1, tiled=True)  73 us
    all_gather x1, waiting for transfers between devices, local(): lax.all_gather(gate_weight, 'dp', axis=0, tiled=True)  69 us
  transfers between devices with their start and end apart: 5, of which 5 were waited for; matrix products, arithmetic and copies ran while one was open for 4% of the time, Pallas kernels for 0%

commit v1 on v0

--- a/solution.py
+++ b/solution.py
@@ -10,7 +10,9 @@
     normed_own = (widened * lax.rsqrt(mean_square + 1e-05) * norm_gain[None, :]).astype(
         jnp.bfloat16
     )
-    normed = lax.all_gather(normed_own, "section", axis=0, tiled=True)
+    normed = jnp.concatenate(
+        lax.all_to_all(jnp.stack([normed_own] * lax.axis_size("section")), "section", 0, 0), axis=0
+    )
     full_gate, full_up, full_down = (
         lax.all_gather(gate_weight, "dp", axis=0, tiled=True),
         lax.all_gather(up_weight, "dp", axis=0, tiled=True),

time: 551 us -> 472 us (0.86)
  waiting for transfers between devices: 503 us -> 314 us
  blocking collectives: 0 us -> 108 us
    all_to_all x0 -> x1, blocking collectives: none -> 108 us  [local(): lax.all_to_all(jnp.stack([normed_own] * lax.axis_size('section')), 'secti...]
    all_gather x1 -> x0, waiting for transfers between devices: 80.9 us -> none  [local(): normed = lax.all_gather(normed_own, 'section', axis=0, tiled=True)]
    all_gather x1, waiting for transfers between devices: 69 us -> 0.01 us  [local(): lax.all_gather(gate_weight, 'dp', axis=0, tiled=True)]
    all_gather x1, waiting for transfers between devices: 73.2 us -> 34.1 us  [local(): lax.all_gather(up_weight, 'dp', axis=0, tiled=True)]
    reshape x0 -> x1, local copies, waits for them, and re-layouts: none -> 6.96 us  [local(): jnp.concatenate(lax.all_to_all(jnp.stack([normed_own] * lax.axis_size('se...]
    unnamed x6 -> x5, local copies, waits for them, and re-layouts: 8.13 us -> 1.23 us
    unnamed x6 -> x5, waiting for transfers between devices: 206 us -> 207 us
  transfers between devices with their start and end apart: 5 -> 4, of which waited for: 5 -> 3; matrix products, arithmetic and copies ran while one was open for 4% -> 5% of each run, Pallas kernels for 0% -> 0%
where the time goes in v1:
time: 472 us
  waiting for transfers between devices  314 us (67%)
  blocking collectives  108 us (23%)
  matrix products  21.8 us (5%)
  between operations  13.8 us (3%)
  local copies, waits for them, and re-layouts  10.2 us (2%)
    unnamed x5, waiting for transfers between devices  207 us
    all_to_all x1, blocking collectives, local(): lax.all_to_all(jnp.stack([normed_own] * lax.axis_size('section')), 'secti...  108 us
    all_gather x1, waiting for transfers between devices, local(): lax.all_gather(down_weight, 'dp', axis=1, tiled=True)  73.2 us
    all_gather x1, waiting for transfers between devices, local(): lax.all_gather(up_weight, 'dp', axis=0, tiled=True)  34.1 us
  transfers between devices with their start and end apart: 4, of which 3 were waited for; matrix products, arithmetic and copies ran while one was open for 5% of the time, Pallas kernels for 0%

profile of v1, /device:TPU:2, one launch (start us, length us, event | category | flops | bytes accessed | tf_op | source)
XLA Modules:
  0.0 471.5 jit_solution(16459609966912231522)
XLA Ops:
  6.5 0.0 all-gather.4.cloned.1.call-start
  6.5 0.7 all-gather.4.cloned.1.call-update
  7.3 0.0 all-gather.6.cloned.1.call-start
  7.3 0.7 all-gather.6.cloned.1.call-update
  8.0 0.0 all-gather.8.cloned.1.call-start
  8.1 0.7 all-gather.8.cloned.1.call-update
  8.7 0.0 all-reduce.3.cloned.1.call-start
  8.8 1.0 fusion.1
  9.8 0.9 fusion.3
  10.8 2.0 stack.2
  12.8 108.1 %all_to_all.5 = bf16[64,4,8192]{2,1,0:T(4,128)(2,1)} all-to-all(bf16[64,4,8192]{2,1,0:T(4,128)(2,1)S(1)} %stack.2), channel_id=1, replica_groups=mesh['section'=64,'dp'=4] {'section'}, dimensions={0} | all-to-all | bytes 8388608 | tf_op jit(solution)/shard_map/all_to_all | solution.py:14
  120.9 7.0 %reshape.14 = bf16[256,8192]{1,0:T(8,128)(2,1)} reshape(bf16[64,4,8192]{2,1,0:T(4,128)(2,1)} %all_to_all.5) | data formatting | bytes 8388608 | tf_op jit(solution)/shard_map/reshape | solution.py:13
  127.9 0.0 all-gather.4.cloned.1.call-done
  127.9 6.6 %fusion.5 = f32[256,448]{0,1:T(8,128)S(1)} fusion(bf16[256,8192]{1,0:T(8,128)(2,1)} %reshape.14, bf16[8192,448]{0,1:T(8,128)(2,1)} %all-gather.4.cloned.1.call-done), kind=kOutput, calls=%fused_computation.10 | convolution fusion | flops 1879048192 | bytes 11993088 | tf_op jit(solution)/shard_map/dot_general | solution.py:21
  134.5 34.1 %all-gather.6.cloned.1.call-done = bf16[8192,448]{0,1:T(8,128)(2,1)} async-done(((bf16[2048,448]{0,1:T(8,128)(2,1)}), bf16[8192,448]{0,1:T(8,128)(2,1)}) %all-gather.6.cloned.1.call-update) | async-done | bytes 7340048 | tf_op jit(solution)/shard_map/all_gather | solution.py:18
  168.6 6.4 %fusion = bf16[256,448]{0,1:T(8,128)(2,1)S(1)} fusion(bf16[256,8192]{1,0:T(8,128)(2,1)} %reshape.14, bf16[8192,448]{0,1:T(8,128)(2,1)} %all-gather.6.cloned.1.call-done, f32[256,448]{0,1:T(8,128)S(1)} %fusion.5), kind=kOutput, calls=%fused_computation.1 | convolution fusion | flops 1879736320 | bytes 12222464 | tf_op jit(solution)/shard_map/dot_general | solution.py:22
  175.0 73.2 %all-gather.8.cloned.1.call-done = bf16[448,8192]{1,0:T(8,128)(2,1)} async-done(((bf16[448,2048]{1,0:T(8,128)(2,1)}), bf16[448,8192]{1,0:T(8,128)(2,1)}) %all-gather.8.cloned.1.call-update) | async-done | bytes 7340048 | tf_op jit(solution)/shard_map/all_gather | solution.py:19
  248.2 8.8 %fusion.6 = f32[256,8192]{1,0:T(8,128)} fusion(bf16[256,448]{0,1:T(8,128)(2,1)S(1)} %fusion, bf16[448,8192]{1,0:T(8,128)(2,1)} %all-gather.8.cloned.1.call-done), kind=kOutput, calls=%fused_computation.11 | convolution fusion | flops 1879048192 | bytes 15958016 | tf_op jit(solution)/shard_map/dot_general | solution.py:25
  257.0 0.0 all-reduce.3.cloned.1.call-update
  257.0 0.6 copy-done.1
  257.6 0.6 dynamic-slice
  258.9 204.5 %all-reduce.3.cloned.1.call-done = f32[256,8192]{1,0:T(8,128)} async-done(((f32[256,8192]{1,0:T(8,128)}), f32[256,8192]{1,0:T(8,128)}) %all-reduce.3.cloned.1.call-update) | async-done | bytes 8388624
  463.4 0.0 copy-done
  463.4 1.6 fusion.4
  (3 shorter events, 0.0 us)
Async XLA Ops:
  6.5 121.4 %all-gather.4.cloned.1.call-start = ((), (), s32[]{:S(2)}) async-start(), calls=%async_computation.1 | async-start | bytes 9175040 | tf_op jit(solution)/shard_map/all_gather | solution.py:17
  7.3 161.3 %all-gather.6.cloned.1.call-start = ((), (), s32[]{:S(2)}) async-start(), calls=%async_computation.2 | async-start | bytes 9175040 | tf_op jit(solution)/shard_map/all_gather | solution.py:18
  8.0 240.2 %all-gather.8.cloned.1.call-start = ((), (), s32[]{:S(2)}) async-start(), calls=%async_computation.3 | async-start | bytes 9175040 | tf_op jit(solution)/shard_map/all_gather | solution.py:19
  8.7 454.6 %all-reduce.3.cloned.1.call-start = ((), (), s32[]{:S(2)}) async-start(), calls=%async_computation.4 | async-start | bytes 16777216
  257.0 0.7 copy-start.1
  257.0 206.4 %copy-start = (bf16[4,8192]{1,0:T(4,128)(2,1)S(1)}, bf16[4,8192]{1,0:T(4,128)(2,1)}, u32[]{:S(2)}) copy-start(bf16[4,8192]{1,0:T(4,128)(2,1)} %param.5) | copy-start | bytes 196612
Sparse Core Ops, SparseCore 0:
  9.2 79.7 all-gather.3
  90.7 77.7 all-gather.5
  170.4 77.7 all-gather.7
  257.1 206.2 all-reduce.2

commit v2 on v0

--- a/solution.py
+++ b/solution.py
@@ -2,6 +2,14 @@
 import jax.numpy as jnp
 from jax import lax
 from jax.sharding import PartitionSpec as P
+
+
+def tiled_gather(shard, axis, dim):
+    peers = lax.axis_size(axis)
+    repeats = [peers if d == dim else 1 for d in range(shard.ndim)]
+    return lax.all_to_all(
+        jnp.tile(shard, repeats), axis, split_axis=dim, concat_axis=dim, tiled=True
+    )
 
 
 def local(tokens, norm_gain, gate_weight, up_weight, down_weight):
@@ -14,7 +22,7 @@
     full_gate, full_up, full_down = (
         lax.all_gather(gate_weight, "dp", axis=0, tiled=True),
         lax.all_gather(up_weight, "dp", axis=0, tiled=True),
-        lax.all_gather(down_weight, "dp", axis=1, tiled=True),
+        tiled_gather(down_weight, "dp", 1),
     )
     gate_part = jnp.dot(normed, full_gate, preferred_element_type=jnp.float32)
     up_part = jnp.dot(normed, full_up, preferred_element_type=jnp.float32)

time: 551 us -> 478 us (0.87)
  waiting for transfers between devices: 503 us -> 333 us
  blocking collectives: 0 us -> 85.9 us
  local copies, waits for them, and re-layouts: 8.13 us -> 18.4 us
    all_to_all x0 -> x1, blocking collectives: none -> 85.9 us  [tiled_gather(): lax.all_to_all(jnp.tile(shard, repeats), axis, split_axis=dim, concat_axi...]
    all_gather x1, waiting for transfers between devices: 80.9 us -> 0.01 us  [local(): normed = lax.all_gather(normed_own, 'section', axis=0, tiled=True)]
    all_gather x1 -> x0, waiting for transfers between devices: 73 us -> none  [local(): lax.all_gather(down_weight, 'dp', axis=1, tiled=True)]
    all_gather x1, waiting for transfers between devices: 69 us -> 54.4 us  [local(): lax.all_gather(gate_weight, 'dp', axis=0, tiled=True)]
    unnamed x6 -> x5, waiting for transfers between devices: 206 us -> 206 us
  transfers between devices with their start and end apart: 5 -> 4, of which waited for: 5 -> 3; matrix products, arithmetic and copies ran while one was open for 4% -> 5% of each run, Pallas kernels for 0% -> 0%
where the time goes in v2:
time: 478 us; the launch traced here: 477 us
  waiting for transfers between devices  333 us (70%)
  blocking collectives  85.9 us (18%)
  matrix products  21.6 us (5%)
  local copies, waits for them, and re-layouts  18.4 us (4%)
  between operations  13.8 us (3%)
    unnamed x5, waiting for transfers between devices  206 us
    all_to_all x1, blocking collectives, tiled_gather(): lax.all_to_all(jnp.tile(shard, repeats), axis, split_axis=dim, concat_axi...  85.9 us
    all_gather x1, waiting for transfers between devices, local(): lax.all_gather(up_weight, 'dp', axis=0, tiled=True)  73.2 us
    all_gather x1, waiting for transfers between devices, local(): lax.all_gather(gate_weight, 'dp', axis=0, tiled=True)  54.4 us
  transfers between devices with their start and end apart: 4, of which 3 were waited for; matrix products, arithmetic and copies ran while one was open for 5% of the time, Pallas kernels for 0%

profile of v2, /device:TPU:2, one launch (start us, length us, event | category | flops | bytes accessed | tf_op | source)
XLA Modules:
  0.0 477.4 jit_solution(16485420358006319867)
XLA Ops:
  6.5 0.0 all-gather.9.cloned.1.call-start
  6.5 1.0 fusion.1
  7.6 1.6 fusion.5
  9.1 0.0 all-gather.9.cloned.1.call-update
  9.2 0.0 all-gather.5.cloned.1.call-start
  9.2 0.7 all-gather.5.cloned.1.call-update
  9.9 0.0 all-gather.7.cloned.1.call-start
  10.0 0.7 all-gather.7.cloned.1.call-update
  10.7 0.0 all-reduce.3.cloned.1.call-start
  10.7 5.4 %tile.2 = bf16[448,4,2048]{2,0,1:T(8,128)(2,1)} broadcast(bf16[448,2048]{1,0:T(8,128)(2,1)} %param.9), dimensions={0,2} | broadcast | bytes 9175040 | tf_op jit(solution)/shard_map/tile | solution.py:11
  16.1 85.9 %all_to_all.9 = bf16[448,4,2048]{2,0,1:T(8,128)(2,1)S(1)} all-to-all(bf16[448,4,2048]{2,0,1:T(8,128)(2,1)} %tile.2), channel_id=1, replica_groups=mesh['section'=64,'dp'=4] {'dp'}, dimensions={1} | all-to-all | bytes 14680064 | tf_op jit(solution)/shard_map/all_to_all | solution.py:10
  102.0 4.7 copy.7
  106.7 7.0 %reshape.17 = bf16[256,8192]{1,0:T(8,128)(2,1)} reshape(bf16[64,4,8192]{2,1,0:T(4,128)(2,1)} %all-gather.9.cloned.1.call-done) | data formatting | bytes 8388608
  113.7 54.4 %all-gather.5.cloned.1.call-done = bf16[8192,448]{0,1:T(8,128)(2,1)} async-done(((bf16[2048,448]{0,1:T(8,128)(2,1)}), bf16[8192,448]{0,1:T(8,128)(2,1)}) %all-gather.5.cloned.1.call-update) | async-done | bytes 7340048 | tf_op jit(solution)/shard_map/all_gather | solution.py:23
  168.1 6.4 %fusion.6 = f32[256,448]{0,1:T(8,128)S(1)} fusion(bf16[256,8192]{1,0:T(8,128)(2,1)} %reshape.17, bf16[8192,448]{0,1:T(8,128)(2,1)} %all-gather.5.cloned.1.call-done), kind=kOutput, calls=%fused_computation.11 | convolution fusion | flops 1879048192 | bytes 11993088 | tf_op jit(solution)/shard_map/dot_general | solution.py:27
  174.5 73.2 %all-gather.7.cloned.1.call-done = bf16[8192,448]{0,1:T(8,128)(2,1)} async-done(((bf16[2048,448]{0,1:T(8,128)(2,1)}), bf16[8192,448]{0,1:T(8,128)(2,1)}) %all-gather.7.cloned.1.call-update) | async-done | bytes 7340048 | tf_op jit(solution)/shard_map/all_gather | solution.py:24
  247.7 6.5 %fusion = bf16[256,448]{0,1:T(8,128)(2,1)S(1)} fusion(bf16[256,8192]{1,0:T(8,128)(2,1)} %reshape.17, bf16[8192,448]{0,1:T(8,128)(2,1)} %all-gather.7.cloned.1.call-done, f32[256,448]{0,1:T(8,128)S(1)} %fusion.6), kind=kOutput, calls=%fused_computation.1 | convolution fusion | flops 1879736320 | bytes 12222464 | tf_op jit(solution)/shard_map/dot_general | solution.py:28
  254.2 8.7 %fusion.7 = f32[256,8192]{1,0:T(8,128)} fusion(bf16[256,448]{0,1:T(8,128)(2,1)S(1)} %fusion, bf16[448,8192]{1,0:T(8,128)(2,1)} %bitcast.11), kind=kOutput, calls=%fused_computation.12 | convolution fusion | flops 1879048192 | bytes 15958016 | tf_op jit(solution)/shard_map/dot_general | solution.py:31
  262.9 0.0 all-reduce.3.cloned.1.call-update
  262.9 0.6 copy-done.1
  263.5 0.6 dynamic-slice
  264.8 204.5 %all-reduce.3.cloned.1.call-done = f32[256,8192]{1,0:T(8,128)} async-done(((f32[256,8192]{1,0:T(8,128)}), f32[256,8192]{1,0:T(8,128)}) %all-reduce.3.cloned.1.call-update) | async-done | bytes 8388624
  469.3 0.0 copy-done
  469.3 1.6 fusion.4
  (4 shorter events, 0.0 us)
Async XLA Ops:
  6.5 100.1 %all-gather.9.cloned.1.call-start = ((), (), s32[]{:S(2)}) async-start(), calls=%async_computation.3 | async-start | bytes 4259840 | tf_op jit(solution)/shard_map/all_gather | solution.py:21
  9.2 158.9 %all-gather.5.cloned.1.call-start = ((), (), s32[]{:S(2)}) async-start(), calls=%async_computation.1 | async-start | bytes 9175040 | tf_op jit(solution)/shard_map/all_gather | solution.py:23
  9.9 237.8 %all-gather.7.cloned.1.call-start = ((), (), s32[]{:S(2)}) async-start(), calls=%async_computation.2 | async-start | bytes 9175040 | tf_op jit(solution)/shard_map/all_gather | solution.py:24
  10.7 458.6 %all-reduce.3.cloned.1.call-start = ((), (), s32[]{:S(2)}) async-start(), calls=%async_computation.4 | async-start | bytes 16777216
  262.9 0.7 copy-start.1
  262.9 206.4 %copy-start = (bf16[4,8192]{1,0:T(4,128)(2,1)S(1)}, bf16[4,8192]{1,0:T(4,128)(2,1)}, u32[]{:S(2)}) copy-start(bf16[4,8192]{1,0:T(4,128)(2,1)} %param.5) | copy-start | bytes 196612
Sparse Core Ops, SparseCore 0:
  10.1 81.9 all-gather.8
  94.0 74.0 all-gather.4
  169.9 77.7 all-gather.6
  263.0 206.2 all-reduce.2
